TPU v7x, 32 devices: a whole 2x2x4 slice. The times are simulated.
32 devices in a mesh: vocab: 8 (over z, y), feat: 4 (over x, core).
Axes of the slice: x: 2, y: 2, z: 4, core: 2. Of those that a mesh axis runs over, the one named last changes fastest.
Arguments:
- hidden: bfloat16 [1024, 4096], P('feat'), may hold values from -64 to 64
- out_head: bfloat16 [32768, 4096], P(('vocab', 'feat')), may hold values from -0.28125 to 0.28125
- out_proj: bfloat16 [32768, 128], P(('vocab', 'feat')), may hold values from -5 to 5
- in_proj: bfloat16 [4096, 128], replicated, may hold values from -0.09375 to 0.09375
- targets: int32 [1024], replicated, may hold values from 0 to 32767
- seq_ids: int32 [1024], replicated, may hold values from 0 to 15, never falling along the last dimension, each value on 1 to 128 neighbouring positions
- grad_store: bfloat16 [16384, 16384], P('vocab', 'feat'), may hold values from -0.01953125 to 0.01953125
Outputs:
- influence: float32 [16384, 16], P(('vocab', 'feat'))
All inputs are finite; a program needn't handle non-finite values.
Results may differ from a plain program's by a relative error of at most 0.003.
Values may be sent and summed in bfloat16 or wider, within the bound.
A program may use at most 128 MiB of HBM per device.

v0:
```python
import functools

import jax
import jax.numpy as jnp
from jax import lax
from jax.experimental import pallas as pl
from jax.experimental.pallas import tpu as pltpu
from jax.sharding import PartitionSpec as P

SEQS = 16
SUBS = 4
F32 = jnp.float32
BF16 = jnp.bfloat16
NT = (((1,), (1,)), ((), ()))


def kernel(nv, nf, hid_in, head_in, oproj, iproj_in, targets, seqs, gs_in, out,
           hid, head, iproj, gs, lg, o_t, o_full, ins, sv, so, s2, st, rv, r1, ro, rst, osb, qg, qgm, part, infl,
           load_sem, x_send, y_send, z_send, s_send, recv, s_recv, own_sems,
           sv_send, so_send, s2_send, st_send, rv_sem, r1_sem, ro_sem, rst_sem, ag_send, ag_recv, in_send, in_recv, loc_sem, heard):
    v = lax.axis_index("vocab")
    f = lax.axis_index("feat")
    me = v * nf + f
    nd = nv * nf
    x, k = f // 2, f % 2
    xn = nf // 2
    sib = f + 1 - 2 * k
    vy = v + 1 - 2 * (v % 2)
    vz = v + 2 - 4 * ((v // 2) % 2)
    vd = vy + vz - v
    vl = head.shape[0]
    rank = oproj.shape[1]
    rf, tb = sv.shape[1], sv.shape[2]
    parts = hid.shape[1]
    tc = 2 * tb
    eo = out.shape[1]
    piece = tb // 4
    per = SUBS // parts
    sr = piece // per

    loads = [
        pltpu.make_async_copy(head_in, head, load_sem.at[0]),
        pltpu.make_async_copy(iproj_in, iproj, load_sem.at[1]),
        pltpu.make_async_copy(gs_in, gs, load_sem.at[2]),
    ]

    def half(xi, kk, h):
        return hid.at[xi, h, pl.ds(pl.multiple_of(kk * tb, tb), tb)]

    mine = [pltpu.make_async_copy(hid_in.at[pl.ds(h * tb, tb)], half(x, k, h), load_sem.at[3 + h])
            for h in range(parts)]
    for copy in mine + loads[:2]:
        copy.start()

    def flip(i, bit):
        return i + bit - 2 * bit * ((i // bit) % 2)

    near = [(v, flip(f, 1 << i)) for i in range(nf.bit_length() - 1)]
    near += [(flip(v, 1 << i), f) for i in range(nv.bit_length() - 1)]
    barrier = pltpu.get_barrier_semaphore()

    def signal(sem, place):
        pl.semaphore_signal(sem, inc=1, device_id={"vocab": place[0], "feat": place[1]},
                            device_id_type=pl.DeviceIdType.MESH)

    for place in near:
        signal(barrier, place)
    pl.semaphore_wait(barrier, len(near))

    def hear(lo, hi):
        for i in range(lo, hi):
            signal(heard.at[i], near[i])
            pl.semaphore_wait(heard.at[i], 1)

    hear(0, nf.bit_length() - 1)

    def remote(src, dst, ss, rs, dv, df):
        return pltpu.make_async_remote_copy(
            src_ref=src, dst_ref=dst, send_sem=ss, recv_sem=rs,
            device_id={"vocab": dv, "feat": df}, device_id_type=pl.DeviceIdType.MESH)

    def rows(xi, kk, owner, j):
        at = kk * tb + (owner % 4) * piece + (j % per) * sr
        return hid.at[xi, j // per, pl.ds(pl.multiple_of(at, sr), sr)]

    pending = []

    def go(copy):
        copy.start()
        pending.append(copy)

    for h in range(parts):
        mine[h].wait()
        for r in range(xn - 1):
            fo = 2 * ((x + r + 1) % xn) + k
            for j in range(h * per, (h + 1) * per):
                blk = rows(x, k, v, j)
                go(remote(blk, blk, x_send.at[r, j], recv.at[r, 0, j], v, fo))
        if h == parts - 1:
            for r in range(xn - 1):
                fo = 2 * ((x + r + 1) % xn) + k
                for j in range(h * per, (h + 1) * per):
                    blk = rows(x, k, vd, j)
                    go(remote(blk, blk, x_send.at[r, j + per], recv.at[r, 3, j], v, fo))
        go(remote(half(x, k, h), half(x, k, h), own_sems.at[0, h], own_sems.at[1, h], v, sib))
    loads[2].start()

    def src_of(r):
        return (x + xn - r - 1) % xn

    owners = (v, vy, vz, vd)

    def arrive(r, rel, j):
        blk = rows(src_of(r), k, owners[rel], j)
        remote(blk, blk, x_send.at[r, j], recv.at[r, rel, j], v, f).wait_recv()
        first = j % per < per // 2
        relay = j // per < parts - 1
        if rel == 0:
            go(remote(blk, blk, y_send.at[r, 0, j], recv.at[r, 1, j], vy, f))
            go(remote(blk, blk, z_send.at[r, 0, j], recv.at[r, 2, j], vz, f))
        if rel == 1 and relay and first:
            go(remote(blk, blk, z_send.at[r, 1, j], recv.at[r, 3, j], vz, f))
        if rel == 2 and relay and not first:
            go(remote(blk, blk, y_send.at[r, 1, j], recv.at[r, 3, j], vy, f))
        go(remote(blk, blk, s_send.at[r, rel, j], s_recv.at[r, rel, j], v, sib))

    def post(send_buf, recv_buf, sends, recvs, d):
        @pl.when(d != me)
        def _():
            remote(send_buf, recv_buf, sends.at[d], recvs.at[me], d // nf, d % nf).start()

    o_t[...] = oproj[...].astype(F32).T.astype(BF16)
    base = me * vl

    def onehot_step(c, carry):
        xi, h = c // parts, c % parts
        blks = [(2 * xi + kk) * parts + h for kk in range(2)]
        ids = lax.broadcasted_iota(jnp.int32, (vl, tc), 0) + base
        goal = jnp.concatenate([targets[b] for b in blks], axis=1)
        hot = (goal == ids).astype(F32).astype(BF16)
        o = jnp.dot(o_t[...], hot, preferred_element_type=F32)
        o_full[c] = o
        for kk in range(2):
            for g in range(nf):
                so[g, blks[kk]] = o[g * rf:(g + 1) * rf, kk * tb:(kk + 1) * tb].astype(BF16)
        return carry

    lax.fori_loop(0, xn * parts, onehot_step, 0)
    hear(nf.bit_length() - 1, len(near))
    for p in range(1, nf):
        g = (f + p) % nf
        go(remote(so.at[g], r1.at[f], so_send.at[p], r1_sem.at[f], v, g))

    def onehot_sum():
        for p in range(1, nf):
            g = (f + p) % nf
            remote(so.at[g], r1.at[g], so_send.at[p], r1_sem.at[g], v, g).wait_recv()

        def one(b, c):
            t = so[f, b].astype(F32)
            for p in range(1, nf):
                t = t + r1[(f + p) % nf, b].astype(F32)
            s2[b] = t.astype(BF16)
            return c

        lax.fori_loop(0, nv, one, 0)
        for p in range(1, nv):
            b = (v + p) % nv
            go(remote(s2.at[b], ro.at[v], s2_send.at[p], ro_sem.at[v], b, f))

    vt = min(256, vl)
    nt = vl // vt

    def tiles(xi, h, lo, hi, m):
        def tile(i, m):
            at = pl.ds(pl.multiple_of(i * vt, vt), vt)
            l = lax.dot_general(head[at, :], hid[xi, h], NT, preferred_element_type=F32)
            lg[at, :] = l
            return jnp.maximum(m, jnp.max(l, axis=0, keepdims=True))
        return lax.fori_loop(lo, hi, tile, m)

    def finish(xi, h, m):
        e = jnp.exp(lg[...] - m)
        s = jnp.sum(e, axis=0, keepdims=True)
        u = jnp.dot(o_t[...], e.astype(BF16), preferred_element_type=F32)
        u = u / s - o_full[xi * parts + h]
        blks = [(2 * xi + kk) * parts + h for kk in range(2)]
        for kk in range(2):
            lanes = slice(kk * tb, (kk + 1) * tb)
            st[blks[kk], 0:1, :] = m[:, lanes]
            st[blks[kk], 1:2, :] = s[:, lanes]
            for g in range(nf):
                sv[blks[kk] * nf + g] = u[g * rf:(g + 1) * rf, lanes].astype(BF16)
        for kk in range(2):
            for g in range(nf):
                d = blks[kk] * nf + g
                post(st.at[blks[kk]], rst.at[me], st_send, rst_sem, d)
                post(sv.at[d], rv.at[me], sv_send, rv_sem, d)
        act = jnp.dot(hid[xi, h], iproj[...], preferred_element_type=F32)
        for kk in range(2):
            ins[blks[kk]] = act[kk * tb:(kk + 1) * tb]

    low = jnp.full((1, tc), -jnp.inf, F32)
    every = range(xn - 1)

    def sibling(h):
        blk = half(x, 1 - k, h)
        remote(blk, blk, own_sems.at[0, h], own_sems.at[1, h], v, sib).wait_recv()

    def arrivals(*which):
        for rel, j in which:
            for r in every:
                arrive(r, rel, j)

    def passed(r, h):
        for rel in range(4):
            for j in range(h * per, (h + 1) * per):
                blk = rows(src_of(r), 1 - k, owners[rel], j)
                remote(blk, blk, s_send.at[r, rel, j], s_recv.at[r, rel, j], v, sib).wait_recv()

    mid = nt // 2
    loads[0].wait()
    loads[1].wait()
    sibling(0)
    arrivals((0, 0))
    m = tiles(x, 0, 0, mid, low)
    arrivals((0, 1))
    m = tiles(x, 0, mid, nt, m)
    arrivals((1, 0), (2, 0), (0, 2))
    finish(x, 0, m)
    sibling(1)
    m = tiles(x, 1, 0, mid, low)
    arrivals((1, 1), (2, 1), (0, 3))
    m = tiles(x, 1, mid, nt, m)
    finish(x, 1, m)
    onehot_sum()
    arrivals((3, 0), (3, 1))
    for r in every:
        passed(r, 0)
        m = tiles(src_of(r), 0, 0, mid, low)
        if r == 0:
            arrivals((1, 2), (2, 2))
        m = tiles(src_of(r), 0, mid, nt, m)
        finish(src_of(r), 0, m)
    arrivals((3, 2), (3, 3), (1, 3), (2, 3))
    for r in every:
        passed(r, 1)
        finish(src_of(r), 1, tiles(src_of(r), 1, 0, nt, low))

    local = [pltpu.make_async_copy(sv.at[me], rv.at[me], loc_sem.at[0]),
             pltpu.make_async_copy(st.at[v], rst.at[me], loc_sem.at[1])]
    for copy in local:
        copy.start()
    targeted = s2[v].astype(F32)
    for p in range(1, nv):
        b = (v + p) % nv
        remote(s2.at[b], ro.at[b], s2_send.at[p], ro_sem.at[b], v, f).wait_recv()
        targeted = targeted + ro[b].astype(F32)
    for copy in local:
        copy.wait()

    def take(p, c):
        d = (me + p) % nd
        remote(st.at[v], rst.at[d], st_send.at[d], rst_sem.at[d], v, f).wait_recv()
        remote(sv.at[d], rv.at[d], sv_send.at[d], rv_sem.at[d], v, f).wait_recv()
        return c

    lax.fori_loop(1, nd, take, 0)
    peak, mass = rst[:, 0, :], rst[:, 1, :]
    mass = jnp.exp(peak - jnp.max(peak, axis=0, keepdims=True)) * mass
    share = mass / jnp.sum(mass, axis=0, keepdims=True)
    first_row = lax.broadcasted_iota(jnp.int32, (nd, tb), 0) * vl
    goal = targets[v]
    outside = (goal < first_row) | (goal >= first_row + vl)
    acc = -jnp.sum(jnp.where(outside, share, 0.0), axis=0, keepdims=True) * targeted
    for d in range(nd):
        w = share[d:d + 1, :]
        acc = acc + w * rv[d].astype(F32)
    osb[v] = acc

    def spread(p, c):
        dv = (v + p) % nv
        remote(osb.at[v], osb.at[v], ag_send.at[p], ag_recv.at[v], dv, f).start()
        return c

    lax.fori_loop(1, nv, spread, 0)

    qg[...] = jnp.zeros_like(qg)

    def outer(p, c):
        b = (v + p) % nv

        @pl.when(p > 0)
        def _():
            remote(osb.at[b], osb.at[b], ag_send.at[p], ag_recv.at[b], v, f).wait_recv()

        member = (seqs[b] == lax.broadcasted_iota(jnp.int32, (SEQS, tb), 0)).astype(F32)
        o = osb[b]
        weighted = jnp.concatenate([member * o[i:i + 1, :] for i in range(rf)], axis=0)
        qg[...] += jnp.dot(weighted, ins[b], preferred_element_type=F32, precision=lax.Precision.HIGHEST)
        return c

    lax.fori_loop(0, nv, outer, 0)
    for i in range(rf):
        qgm[:, i * rank:(i + 1) * rank] = qg[i * SEQS:(i + 1) * SEQS, :].astype(BF16)
    loads[2].wait()

    def score(p, c):
        t = p + 1
        g = 2 * ((x + t // 2) % xn) + (k + 1 + t % 2) % 2
        part[g] = lax.dot_general(
            qgm[...], gs[pl.ds(pl.multiple_of(g * eo, eo), eo), :], NT, preferred_element_type=F32)

        @pl.when(p < nf)
        def _():
            remote(part.at[g], infl.at[f], in_send.at[p % nf], in_recv.at[f], v, g).start()
        return c

    lax.fori_loop(1, nf + 1, score, 0)
    result = part[f]
    for p in range(1, nf):
        g = (f + p) % nf
        remote(part.at[g], infl.at[g], in_send.at[p], in_recv.at[g], v, g).wait_recv()
        result = result + infl[g]
    out[...] = result

    for copy in pending:
        copy.wait_send()

    def drain(p, c):
        d = (me + p) % nd
        remote(st.at[d // nf], rst.at[me], st_send.at[d], rst_sem.at[me], v, f).wait_send()
        remote(sv.at[d], rv.at[me], sv_send.at[d], rv_sem.at[me], v, f).wait_send()
        return c

    lax.fori_loop(1, nd, drain, 0)
    for p in range(1, nv):
        remote(osb.at[v], osb.at[v], ag_send.at[p], ag_recv.at[v], v, f).wait_send()
    for p in range(1, nf):
        g = (f + p) % nf
        remote(part.at[g], infl.at[f], in_send.at[p], in_recv.at[f], v, f).wait_send()


def solution(mesh):
    nv, nf = mesh.shape["vocab"], mesh.shape["feat"]
    nd = nv * nf
    xn = nf // 2

    def on_device(hidden, out_head, out_proj, in_proj, targets, seq_ids, grad_store):
        tl, width = hidden.shape
        vl, rank = out_proj.shape
        el, fl = grad_store.shape
        tokens = tl * nf
        rf, tb, eo = rank // nf, tokens // nv, el // nf
        parts = tl // tb
        any_spec = pl.BlockSpec(memory_space=pl.ANY)
        vmem = pl.BlockSpec(memory_space=pltpu.VMEM)
        dma = pltpu.SemaphoreType.DMA
        res = pl.pallas_call(
            functools.partial(kernel, nv, nf),
            out_shape=jax.ShapeDtypeStruct((SEQS, eo), F32),
            in_specs=[any_spec, any_spec, vmem, any_spec, vmem, vmem, any_spec],
            out_specs=vmem,
            scratch_shapes=[
                pltpu.VMEM((xn, parts, 2 * tb, width), BF16),
                pltpu.VMEM((vl, width), BF16),
                pltpu.VMEM((width, rank), BF16),
                pltpu.VMEM((el, fl), BF16),
                pltpu.VMEM((vl, 2 * tb), F32),
                pltpu.VMEM((rank, vl), BF16),
                pltpu.VMEM((xn * parts, rank, 2 * tb), F32),
                pltpu.VMEM((nv, tb, rank), F32),
                pltpu.VMEM((nd, rf, tb), BF16),
                pltpu.VMEM((nf, nv, rf, tb), BF16),
                pltpu.VMEM((nv, rf, tb), BF16),
                pltpu.VMEM((nv, 2, tb), F32),
                pltpu.VMEM((nd, rf, tb), BF16),
                pltpu.VMEM((nf, nv, rf, tb), BF16),
                pltpu.VMEM((nv, rf, tb), BF16),
                pltpu.VMEM((nd, 2, tb), F32),
                pltpu.VMEM((nv, rf, tb), F32),
                pltpu.VMEM((rf * SEQS, rank), F32),
                pltpu.VMEM((SEQS, fl), BF16),
                pltpu.VMEM((nf, SEQS, eo), F32),
                pltpu.VMEM((nf, SEQS, eo), F32),
                dma((3 + parts,)),
                dma((xn - 1, SUBS + SUBS // parts)),
                dma((xn - 1, 2, SUBS)),
                dma((xn - 1, 2, SUBS)),
                dma((xn - 1, 4, SUBS)),
                dma((xn - 1, 4, SUBS)),
                dma((xn - 1, 4, SUBS)),
                dma((2, parts)),
                dma((nd,)),
                dma((nf,)),
                dma((nv,)),
                dma((nd,)),
                dma((nd,)),
                dma((nf,)),
                dma((nv,)),
                dma((nd,)),
                dma((nv,)),
                dma((nv,)),
                dma((nf,)),
                dma((nf,)),
                dma((2,)),
                pltpu.SemaphoreType.REGULAR((nf.bit_length() + nv.bit_length() - 2,)),
            ],
            compiler_params=pltpu.CompilerParams(
                collective_id=0, has_side_effects=True, vmem_limit_bytes=60 * 1024 * 1024),
        )(hidden, out_head, out_proj, in_proj, targets.reshape(nv, 1, tb), seq_ids.reshape(nv, 1, tb), grad_store)
        return res.T

    in_specs = (
        P("feat", None),
        P(("vocab", "feat"), None),
        P(("vocab", "feat"), None),
        P(),
        P(),
        P(),
        P("vocab", "feat"),
    )
    return jax.shard_map(
        on_device, mesh=mesh, in_specs=in_specs, out_specs=P(("vocab", "feat"), None), check_vma=False
    )
```

profile of v0, /device:TPU:0, one launch (start us, length us, event | category | flops | bytes accessed | tf_op | source)
XLA Modules:
  0.0 62.0 jit_solution(15221097613084357324)
XLA Ops:
  0.0 60.6 %shard_map.73 = f32[16,512]{1,0:T(8,128)} custom-call(bf16[256,4096]{1,0:T(8,128)(2,1)} %hid_in.1, bf16[1024,4096]{1,0:T(8,128)(2,1)} %head_in.1, bf16[1024,128]{1,0:T(8,128)(2,1)} %oproj.1, bf16[4096,128]{1,0:T(8,128)(2,1)} %iproj_in.1, s32[8,1,128]{2,1,0:T(1,128)} %bitcast.4, s32[8,1,128]{2,1,0:T(1,128)} %bitcast.5, bf16[2048,4096]{1,0:T(8,128)(2,1)} %gs_in.1), custom_call_target="tpu_custom_call" | custom-call | tf_op jit(solution)/shard_map/pallas_call | solution.py:359
  60.6 1.4 %copy.9 = f32[512,16]{0,1:T(8,128)} copy(f32[512,16]{0,1:T(8,128)} %bitcast.3) | data formatting | bytes 65536
where the time goes:
time: 62.2 us; the launch traced here: 62 us
  Pallas kernels  60.6 us (97%)
  local copies, waits for them, and re-layouts  1.38 us (2%)
    pallas_call x1, Pallas kernels, on_device(): pl.pallas_call(functools.partial(kernel, nv, nf), out_shape=jax.ShapeDtyp...  60.6 us
    unnamed x1, local copies, waits for them, and re-layouts  1.38 us

commit v1 on v0

v1 whole, which is shorter than its diff:
```python
import functools

import jax
import jax.numpy as jnp
from jax import lax
from jax.experimental import pallas as pl
from jax.experimental.pallas import tpu as pltpu
from jax.sharding import PartitionSpec as P

SEQS = 16
SUBS = 8
F32 = jnp.float32
BF16 = jnp.bfloat16
NT = (((1,), (1,)), ((), ()))


def kernel(nv, nf, hid_in, head_in, oproj_in, iproj_in, targets_in, seqs_in, gs_in, out,
           hid, head, oproj, iproj, targets, seqs, gs, lg, o_t, o_full, ins, sv, so, s2, st, rv, r0, r1, ro, rst, osb,
           qg, qgm, part, infl,
           load_sem, x_send, y_send, z_send, s_send, own_send, recv, s_recv, own_recv, so_sem, ox_send, ox_recv, ro_sem,
           sv_sem, st_sem, ag_send, ag_recv, in_sem, loc_sem, heard):
    v = lax.axis_index("vocab")
    f = lax.axis_index("feat")
    me = v * nf + f
    nd = nv * nf
    x, k = f // 2, f % 2
    xn = nf // 2
    sib = f + 1 - 2 * k
    vy = v + 1 - 2 * (v % 2)
    vz = v + 2 - 4 * ((v // 2) % 2)
    vd = vy + vz - v
    vl = head.shape[0]
    width = head.shape[1]
    rank = oproj.shape[1]
    rf, tb = sv.shape[1], sv.shape[2]
    parts = hid.shape[1]
    tc = 2 * tb
    eo = out.shape[1]
    piece = tb // 4
    per = SUBS // parts
    sr = 2 * piece // per
    quarter = nv // 4

    def owner(h, i):
        spot = (1 - i % 2) * (i // 2) + (i % 2) * (2 * quarter - 1 - i // 2)
        return quarter + spot if h else spot + 2 * quarter * (spot // quarter)

    def block(w):
        late = ((w // quarter + 1) // 2) % 2
        spot = late * (w - quarter) + (1 - late) * (w - 2 * quarter * (w // (2 * quarter)))
        i = (1 - spot // quarter) * 2 * spot + (spot // quarter) * (4 * quarter - 1 - 2 * spot)
        return 2 * i + late

    mb = block(v)

    loads = [
        pltpu.make_async_copy(oproj_in, oproj, load_sem.at[0]),
        pltpu.make_async_copy(targets_in, targets, load_sem.at[1]),
        pltpu.make_async_copy(head_in, head, load_sem.at[2]),
        pltpu.make_async_copy(iproj_in, iproj, load_sem.at[3]),
        pltpu.make_async_copy(seqs_in, seqs, load_sem.at[4]),
        pltpu.make_async_copy(gs_in, gs, load_sem.at[5]),
    ]

    def half(xi, kk, h):
        return hid.at[xi, h, pl.ds(pl.multiple_of(kk * tb, tb), tb)]

    mine = [pltpu.make_async_copy(hid_in.at[pl.ds(h * tb, tb)], half(x, k, h), load_sem.at[6 + h])
            for h in range(parts)]

    def flip(i, bit):
        return i + bit - 2 * bit * ((i // bit) % 2)

    near = [(v, flip(f, 1 << i)) for i in range(nf.bit_length() - 1)]
    near += [(flip(v, 1 << i), f) for i in range(nv.bit_length() - 1)]
    barrier = pltpu.get_barrier_semaphore()

    def signal(sem, place):
        pl.semaphore_signal(sem, inc=1, device_id={"vocab": place[0], "feat": place[1]},
                            device_id_type=pl.DeviceIdType.MESH)

    for place in near:
        signal(barrier, place)
    for copy in mine + loads[:5]:
        copy.start()
    with jax.named_scope("barrier"):
        pl.semaphore_wait(barrier, len(near))
    said = [0]

    def hear(upto):
        for i in range(said[0], upto):
            pl.semaphore_wait(heard.at[i], 1)
            if i + 1 < len(near):
                signal(heard.at[i + 1], near[i + 1])
        said[0] = max(said[0], upto)

    signal(heard.at[0], near[0])
    if xn > 2:
        hear(nf.bit_length() - 1)

    def remote(src, dst, ss, rs, dv, df):
        return pltpu.make_async_remote_copy(
            src_ref=src, dst_ref=dst, send_sem=ss, recv_sem=rs,
            device_id={"vocab": dv, "feat": df}, device_id_type=pl.DeviceIdType.MESH)

    def rows(xi, kk, own, j):
        c = j % per
        at = kk * tb + (own % 4) * piece + (c // 2) * sr
        cols = pl.ds((c % 2) * (width // 2), width // 2)
        return hid.at[xi, j // per, pl.ds(pl.multiple_of(at, sr), sr), cols]

    for h in range(parts):
        mine[h].wait()
        for r in range(xn - 1):
            fo = 2 * ((x + r + 1) % xn) + k
            for j in range(h * per, (h + 1) * per):
                blk = rows(x, k, v, j)
                remote(blk, blk, x_send.at[r], recv.at[r, 0, j], v, fo).start()
        if h == parts - 1:
            for r in range(xn - 1):
                fo = 2 * ((x + r + 1) % xn) + k
                for j in range(h * per, (h + 1) * per):
                    blk = rows(x, k, vd, j)
                    remote(blk, blk, x_send.at[r], recv.at[r, 3, j], v, fo).start()
        remote(half(x, k, h), half(x, k, h), own_send, own_recv.at[h], v, sib).start()
    loads[5].start()

    def src_of(r):
        return (x + xn - r - 1) % xn

    owners = (v, vy, vz, vd)

    def arrive(r, rel, j):
        blk = rows(src_of(r), k, owners[rel], j)
        remote(blk, blk, x_send.at[r], recv.at[r, rel, j], v, f).wait_recv()
        relay = j // per < parts - 1
        if rel == 0:
            remote(blk, blk, y_send.at[r], recv.at[r, 1, j], vy, f).start()
            remote(blk, blk, z_send.at[r], recv.at[r, 2, j], vz, f).start()
        if rel == 1 and relay and j % 2 == 0:
            remote(blk, blk, z_send.at[r], recv.at[r, 3, j], vz, f).start()
        if rel == 2 and relay and j % 2 == 1:
            remote(blk, blk, y_send.at[r], recv.at[r, 3, j], vy, f).start()
        remote(blk, blk, s_send.at[r], s_recv.at[r, j // per], v, sib).start()

    def post(send_buf, recv_buf, sem, d):
        @pl.when(d != me)
        def _():
            remote(send_buf, recv_buf, sem.at[0], sem.at[1], d // nf, d % nf).start()

    hear(1)
    loads[0].wait()
    loads[1].wait()
    o_t[...] = oproj[...].astype(F32).T.astype(BF16)
    base = me * vl

    def onehot_step(c, carry):
        xi, h = c // parts, c % parts
        blks = [(2 * xi + kk) * parts + h for kk in range(2)]
        ids = lax.broadcasted_iota(jnp.int32, (vl, tc), 0) + base
        goal = jnp.concatenate([targets[b] for b in blks], axis=1)
        hot = (goal == ids).astype(F32).astype(BF16)
        o = jnp.dot(o_t[...], hot, preferred_element_type=F32)
        o_full[c] = o
        for kk in range(2):
            for g in range(nf):
                so[g % 2, g // 2, blks[kk]] = o[g * rf:(g + 1) * rf, kk * tb:(kk + 1) * tb].astype(BF16)
        return carry

    with jax.named_scope("onehot"):
        lax.fori_loop(0, xn * parts, onehot_step, 0)
    over = remote(so.at[1 - k], r0, so_sem.at[0], so_sem.at[1], v, sib)
    over.start()

    def across(p, g):
        return remote(r0.at[g], r1.at[p - 1], ox_send.at[p - 1], ox_recv.at[p - 1], v, 2 * g + k)

    def onehot_over():
        over.wait_recv()

        def one(b, c):
            for g in range(xn):
                r0[g, b] = r0[g, b] + so[k, g, b]
            return c

        lax.fori_loop(0, nv, one, 0)
        for p in range(1, xn):
            across(p, (x + p) % xn).start()

    def spread_to(p):
        b = block((v + p) % nv)
        return remote(s2.at[b], ro.at[p - 1], ro_sem.at[0], ro_sem.at[1], (v + p) % nv, f)

    def onehot_sum():
        for p in range(1, xn):
            across(p, x).wait_recv()

        def one(b, c):
            t = r0[x, b]
            for p in range(1, xn):
                t = t + r1[p - 1, b]
            s2[b] = t
            return c

        lax.fori_loop(0, nv, one, 0)
        for p in range(1, nv):
            spread_to(p).start()

    def tiles(xi, h, lo, hi, m):
        vt = (hi - lo) // 2

        def tile(i, m):
            at = pl.ds(pl.multiple_of(i * vt, vt), vt)
            l = lax.dot_general(head[at, :], hid[xi, h], NT, preferred_element_type=F32)
            lg[at, :] = l
            return jnp.maximum(m, jnp.max(l, axis=0, keepdims=True))

        with jax.named_scope("tiles"):
            return lax.fori_loop(lo // vt, hi // vt, tile, m)

    def finish(xi, h, m):
        with jax.named_scope("finish"):
            e = jnp.exp(lg[...] - m)
            s = jnp.sum(e, axis=0, keepdims=True)
            u = jnp.dot(o_t[...], e.astype(BF16), preferred_element_type=F32)
            u = u / s - o_full[xi * parts + h]
            own = [owner(h, 2 * xi + kk) for kk in range(2)]
            for kk in range(2):
                lanes = slice(kk * tb, (kk + 1) * tb)
                st[own[kk], 0:1, :] = m[:, lanes]
                st[own[kk], 1:2, :] = s[:, lanes]
                for g in range(nf):
                    sv[own[kk] * nf + g] = u[g * rf:(g + 1) * rf, lanes].astype(BF16)
            for kk in range(2):
                for g in range(nf):
                    d = own[kk] * nf + g
                    post(st.at[own[kk]], rst.at[me], st_sem, d)
                    post(sv.at[d], rv.at[me], sv_sem, d)

    def project(xi, h):
        with jax.named_scope("act"):
            act = jnp.dot(hid[xi, h], iproj[...], preferred_element_type=F32)
            hi = act.astype(BF16)
            lo = (act - hi.astype(F32)).astype(BF16)
            both = jnp.concatenate([hi, lo], axis=1)
            for kk in range(2):
                ins[(2 * xi + kk) * parts + h] = both[kk * tb:(kk + 1) * tb]

    low = jnp.full((1, tc), -jnp.inf, F32)
    every = range(xn - 1)

    def sibling(h):
        blk = half(x, 1 - k, h)
        remote(blk, blk, own_send, own_recv.at[h], v, sib).wait_recv()

    def arrivals(*which):
        with jax.named_scope("arr"):
            for rel, j in which:
                for r in every:
                    arrive(r, rel, j)

    def passed(r, h):
        with jax.named_scope("passed"):
            blk = half(src_of(r), 1 - k, h)
            remote(blk, blk, s_send.at[r], s_recv.at[r, h], v, sib).wait_recv()

    mid = vl // 2
    hear(2)
    loads[2].wait()
    loads[3].wait()
    sibling(0)
    m = tiles(x, 0, 0, mid, low)
    hear(3)
    arrivals((0, 0))
    hear(4)
    m = tiles(x, 0, mid, vl, m)
    arrivals((0, 1))
    with jax.named_scope("hear"):
        hear(len(near))
    finish(x, 0, m)
    arrivals((0, 2), (1, 0), (2, 0))
    sibling(1)
    m = tiles(x, 1, 0, mid, low)
    arrivals((0, 3), (1, 1), (2, 1))
    m = tiles(x, 1, mid, vl, m)
    arrivals((0, 4), (1, 2), (2, 2))
    finish(x, 1, m)
    arrivals((0, 5), (1, 3), (2, 3))
    project(x, 0)
    arrivals((0, 6), (1, 4), (2, 4))
    with jax.named_scope("over"):
        onehot_over()
    arrivals((0, 7), (1, 5), (2, 5), (3, 0), (3, 1))
    project(x, 1)
    arrivals((3, 2), (3, 4), (3, 3))
    for r in every:
        passed(r, 0)
        m = tiles(src_of(r), 0, 0, mid, low)
        if r == 0:
            arrivals((3, 5), (1, 6), (2, 6))
        m = tiles(src_of(r), 0, mid, vl, m)
        if r == 0:
            arrivals((3, 6))
        finish(src_of(r), 0, m)
    arrivals((3, 7), (1, 7), (2, 7))
    for r in every:
        project(src_of(r), 0)
    with jax.named_scope("ohsum"):
        onehot_sum()
    for r in every:
        passed(r, 1)
        finish(src_of(r), 1, tiles(src_of(r), 1, 0, vl, low))
    for r in every:
        project(src_of(r), 1)

    local = [pltpu.make_async_copy(sv.at[me], rv.at[me], loc_sem.at[0]),
             pltpu.make_async_copy(st.at[v], rst.at[me], loc_sem.at[1])]
    for copy in local:
        copy.start()
    loads[4].wait()
    some = ro.at[pl.ds(0, nv - 1)]
    with jax.named_scope("row"):
        remote(some, some, ro_sem.at[0], ro_sem.at[1], v, f).wait_recv()
    targeted = s2[mb].astype(F32)
    for p in range(1, nv):
        targeted = targeted + ro[p - 1].astype(F32)
    for copy in local:
        copy.wait()
    stats, shares = rst.at[pl.ds(0, nd - 1)], rv.at[pl.ds(0, nd - 1)]
    with jax.named_scope("take"):
        remote(stats, stats, st_sem.at[0], st_sem.at[1], v, f).wait_recv()
        remote(shares, shares, sv_sem.at[0], sv_sem.at[1], v, f).wait_recv()
    peak, mass = rst[:, 0, :], rst[:, 1, :]
    mass = jnp.exp(peak - jnp.max(peak, axis=0, keepdims=True)) * mass
    share = mass / jnp.sum(mass, axis=0, keepdims=True)
    first_row = lax.broadcasted_iota(jnp.int32, (nd, tb), 0) * vl
    goal = targets[mb]
    outside = (goal < first_row) | (goal >= first_row + vl)
    acc = -jnp.sum(jnp.where(outside, share, 0.0), axis=0, keepdims=True) * targeted
    for d in range(nd):
        w = share[d:d + 1, :]
        acc = acc + w * rv[d].astype(F32)
    osb[mb] = acc

    with jax.named_scope("spread"):
        for p in range(1, nv):
            remote(osb.at[mb], osb.at[mb], ag_send, ag_recv.at[v], (v + p) % nv, f).start()

    def outer(first, b1, b2):
        for b in (b1, b2):
            w = owner(b % 2, b // 2)

            @pl.when(v != w)
            def _():
                with jax.named_scope("agw"):
                    remote(osb.at[b], osb.at[b], ag_send, ag_recv.at[w], v, f).wait_recv()

        with jax.named_scope("outer"):
            member = jnp.concatenate([seqs[b1], seqs[b2]], axis=1) == lax.broadcasted_iota(jnp.int32, (SEQS, tc), 0)
            member = member.astype(F32)
            o = jnp.concatenate([osb[b1], osb[b2]], axis=1)
            hi = o.astype(BF16).astype(F32)
            lo = o - hi
            w_hi = jnp.concatenate([(member * hi[i:i + 1, :]).astype(BF16) for i in range(rf)], axis=0)
            w_lo = jnp.concatenate([(member * lo[i:i + 1, :]).astype(BF16) for i in range(rf)], axis=0)
            right = jnp.concatenate([ins[b1], ins[b2]], axis=0)
            t = jnp.dot(w_hi, right, preferred_element_type=F32)
            t = t[:, :rank] + t[:, rank:] + jnp.dot(w_lo, right[:, :rank], preferred_element_type=F32)
            qg[...] = t if first else qg[...] + t

    for b in range(0, nv, 4):
        outer(b == 0, b, b + 2)
    for b in range(1, nv, 4):
        outer(False, b, b + 2)
    for i in range(rf):
        qgm[:, i * rank:(i + 1) * rank] = qg[i * SEQS:(i + 1) * SEQS, :].astype(BF16)
    loads[5].wait()

    def score(p, c):
        t = p + 1
        g = 2 * ((x + t // 2) % xn) + (k + 1 + t % 2) % 2
        part[g] = lax.dot_general(
            qgm[...], gs[pl.ds(pl.multiple_of(g * eo, eo), eo), :], NT, preferred_element_type=F32)

        @pl.when(p < nf)
        def _():
            remote(part.at[g], infl.at[p - 1], in_sem.at[0], in_sem.at[1], v, g).start()
        return c

    with jax.named_scope("score"):
        lax.fori_loop(1, nf + 1, score, 0)
    result = part[f]
    with jax.named_scope("inflw"):
        landed = infl.at[pl.ds(0, nf - 1)]
        remote(landed, landed, in_sem.at[0], in_sem.at[1], v, f).wait_recv()
    for p in range(1, nf):
        result = result + infl[p - 1]
    out[...] = result

    def sent(ref, sem):
        remote(ref, ref, sem, sem, v, f).wait_send()

    with jax.named_scope("drain"):
        chunk = sr // 2
        for r in every:
            sent(hid.at[0, 0, pl.ds(0, (SUBS + per) * chunk)], x_send.at[r])
            sent(hid.at[0, 0, pl.ds(0, (SUBS + per // 2) * chunk)], y_send.at[r])
            sent(hid.at[0, 0, pl.ds(0, (SUBS + per // 2) * chunk)], z_send.at[r])
            sent(hid.at[0, 0], s_send.at[r])
        sent(hid.at[0, 0], own_send)
        over.wait_send()
        for p in range(1, xn):
            across(p, x).wait_send()
        sent(some, ro_sem.at[0])
        sent(stats, st_sem.at[0])
        sent(shares, sv_sem.at[0])
        sent(osb.at[pl.ds(0, nv - 1)], ag_send)
        sent(landed, in_sem.at[0])


def solution(mesh):
    nv, nf = mesh.shape["vocab"], mesh.shape["feat"]
    nd = nv * nf
    xn = nf // 2

    def on_device(hidden, out_head, out_proj, in_proj, targets, seq_ids, grad_store):
        tl, width = hidden.shape
        vl, rank = out_proj.shape
        el, fl = grad_store.shape
        tokens = tl * nf
        rf, tb, eo = rank // nf, tokens // nv, el // nf
        parts = tl // tb
        any_spec = pl.BlockSpec(memory_space=pl.ANY)
        vmem = pl.BlockSpec(memory_space=pltpu.VMEM)
        dma = pltpu.SemaphoreType.DMA
        res = pl.pallas_call(
            functools.partial(kernel, nv, nf),
            out_shape=jax.ShapeDtypeStruct((SEQS, eo), F32),
            in_specs=[any_spec] * 7,
            out_specs=vmem,
            scratch_shapes=[
                pltpu.VMEM((xn, parts, 2 * tb, width), BF16),
                pltpu.VMEM((vl, width), BF16),
                pltpu.VMEM((vl, rank), BF16),
                pltpu.VMEM((width, rank), BF16),
                pltpu.VMEM((nv, 1, tb), jnp.int32),
                pltpu.VMEM((nv, 1, tb), jnp.int32),
                pltpu.VMEM((el, fl), BF16),
                pltpu.VMEM((vl, 2 * tb), F32),
                pltpu.VMEM((rank, vl), BF16),
                pltpu.VMEM((xn * parts, rank, 2 * tb), F32),
                pltpu.VMEM((nv, tb, 2 * rank), BF16),
                pltpu.VMEM((nd, rf, tb), BF16),
                pltpu.VMEM((2, xn, nv, rf, tb), BF16),
                pltpu.VMEM((nv, rf, tb), BF16),
                pltpu.VMEM((nv, 2, tb), F32),
                pltpu.VMEM((nd, rf, tb), BF16),
                pltpu.VMEM((xn, nv, rf, tb), BF16),
                pltpu.VMEM((xn - 1, nv, rf, tb), BF16),
                pltpu.VMEM((nv - 1, rf, tb), BF16),
                pltpu.VMEM((nd, 2, tb), F32),
                pltpu.VMEM((nv, rf, tb), F32),
                pltpu.VMEM((rf * SEQS, rank), F32),
                pltpu.VMEM((SEQS, fl), BF16),
                pltpu.VMEM((nf, SEQS, eo), F32),
                pltpu.VMEM((nf - 1, SEQS, eo), F32),
                dma((6 + parts,)),
                dma((xn - 1,)),
                dma((xn - 1,)),
                dma((xn - 1,)),
                dma((xn - 1,)),
                dma,
                dma((xn - 1, 4, SUBS)),
                dma((xn - 1, parts)),
                dma((parts,)),
                dma((2,)),
                dma((xn - 1,)),
                dma((xn - 1,)),
                dma((2,)),
                dma((2,)),
                dma((2,)),
                dma,
                dma((nv,)),
                dma((2,)),
                dma((2,)),
                pltpu.SemaphoreType.REGULAR((nf.bit_length() + nv.bit_length() - 2,)),
            ],
            compiler_params=pltpu.CompilerParams(
                collective_id=0, has_side_effects=True, vmem_limit_bytes=60 * 1024 * 1024),
        )(hidden, out_head, out_proj, in_proj, targets.reshape(nv, 1, tb), seq_ids.reshape(nv, 1, tb), grad_store)
        return res.T

    in_specs = (
        P("feat", None),
        P(("vocab", "feat"), None),
        P(("vocab", "feat"), None),
        P(),
        P(),
        P(),
        P("vocab", "feat"),
    )
    return jax.shard_map(
        on_device, mesh=mesh, in_specs=in_specs, out_specs=P(("vocab", "feat"), None), check_vma=False
    )
```

time: 62.2 us -> 52.8 us (0.85)
  Pallas kernels: 60.6 us -> 51.3 us
    pallas_call x1, Pallas kernels: 60.6 us -> 51.3 us  [on_device(): pl.pallas_call(functools.partial(kernel, nv, nf), out_shape=jax.ShapeDtyp...]
where the time goes in v1:
time: 52.8 us; the launch traced here: 52.6 us
  Pallas kernels  51.3 us (97%)
  local copies, waits for them, and re-layouts  1.38 us (3%)
    pallas_call x1, Pallas kernels, on_device(): pl.pallas_call(functools.partial(kernel, nv, nf), out_shape=jax.ShapeDtyp...  51.3 us
    unnamed x1, local copies, waits for them, and re-layouts  1.38 us

profile of v1, /device:TPU:0, one launch (start us, length us, event | category | flops | bytes accessed | tf_op | source)
XLA Modules:
  0.0 52.6 jit_solution(8971821914953075016)
XLA Ops:
  0.0 51.3 %shard_map.73 = f32[16,512]{1,0:T(8,128)} custom-call(bf16[256,4096]{1,0:T(8,128)(2,1)} %hid_in.1, bf16[1024,4096]{1,0:T(8,128)(2,1)} %head_in.1, bf16[1024,128]{1,0:T(8,128)(2,1)} %oproj_in.1, bf16[4096,128]{1,0:T(8,128)(2,1)} %iproj_in.1, s32[8,1,128]{2,1,0:T(1,128)} %bitcast.4, s32[8,1,128]{2,1,0:T(1,128)} %bitcast.5, bf16[2048,4096]{1,0:T(8,128)(2,1)} %gs_in.1), custom_call_target="tpu_custom_call" | custom-call | tf_op jit(solution)/shard_map/pallas_call | solution.py:436
  51.3 1.4 %copy.9 = f32[512,16]{0,1:T(8,128)} copy(f32[512,16]{0,1:T(8,128)} %bitcast.3) | data formatting | bytes 65536

commit v2 on v1

--- a/solution.py
+++ b/solution.py
@@ -116,12 +116,11 @@
             for j in range(h * per, (h + 1) * per):
                 blk = rows(x, k, v, j)
                 remote(blk, blk, x_send.at[r], recv.at[r, 0, j], v, fo).start()
-        if h == parts - 1:
-            for r in range(xn - 1):
-                fo = 2 * ((x + r + 1) % xn) + k
-                for j in range(h * per, (h + 1) * per):
-                    blk = rows(x, k, vd, j)
-                    remote(blk, blk, x_send.at[r], recv.at[r, 3, j], v, fo).start()
+        for r in range(xn - 1):
+            fo = 2 * ((x + r + 1) % xn) + k
+            for j in range(h * per + per // 2, (h + 1) * per):
+                blk = rows(x, k, vd, j)
+                remote(blk, blk, x_send.at[r], recv.at[r, 3, j], v, fo).start()
         remote(half(x, k, h), half(x, k, h), own_send, own_recv.at[h], v, sib).start()
     loads[5].start()
 
@@ -133,7 +132,7 @@
     def arrive(r, rel, j):
         blk = rows(src_of(r), k, owners[rel], j)
         remote(blk, blk, x_send.at[r], recv.at[r, rel, j], v, f).wait_recv()
-        relay = j // per < parts - 1
+        relay = j % per < per // 2
         if rel == 0:
             remote(blk, blk, y_send.at[r], recv.at[r, 1, j], vy, f).start()
             remote(blk, blk, z_send.at[r], recv.at[r, 2, j], vz, f).start()
@@ -231,11 +230,14 @@
                 st[own[kk], 1:2, :] = s[:, lanes]
                 for g in range(nf):
                     sv[own[kk] * nf + g] = u[g * rf:(g + 1) * rf, lanes].astype(BF16)
-            for kk in range(2):
-                for g in range(nf):
-                    d = own[kk] * nf + g
-                    post(st.at[own[kk]], rst.at[me], st_sem, d)
-                    post(sv.at[d], rv.at[me], sv_sem, d)
+
+    def share_out(xi, h):
+        for kk in range(2):
+            w = owner(h, 2 * xi + kk)
+            for g in range(nf):
+                d = w * nf + g
+                post(st.at[w], rst.at[me], st_sem, d)
+                post(sv.at[d], rv.at[me], sv_sem, d)
 
     def project(xi, h):
         with jax.named_scope("act"):
@@ -275,42 +277,45 @@
     hear(4)
     m = tiles(x, 0, mid, vl, m)
     arrivals((0, 1))
+    finish(x, 0, m)
+    sibling(1)
+    m = tiles(x, 1, 0, mid, low)
+    arrivals((0, 2), (1, 0), (2, 0))
     with jax.named_scope("hear"):
         hear(len(near))
-    finish(x, 0, m)
-    arrivals((0, 2), (1, 0), (2, 0))
-    sibling(1)
-    m = tiles(x, 1, 0, mid, low)
-    arrivals((0, 3), (1, 1), (2, 1))
+    arrivals((0, 3))
     m = tiles(x, 1, mid, vl, m)
-    arrivals((0, 4), (1, 2), (2, 2))
+    arrivals((1, 1), (2, 1), (3, 2))
     finish(x, 1, m)
-    arrivals((0, 5), (1, 3), (2, 3))
     project(x, 0)
-    arrivals((0, 6), (1, 4), (2, 4))
+    arrivals((3, 3), (1, 2), (2, 2))
     with jax.named_scope("over"):
         onehot_over()
-    arrivals((0, 7), (1, 5), (2, 5), (3, 0), (3, 1))
+    arrivals((0, 4), (1, 3), (2, 3))
     project(x, 1)
-    arrivals((3, 2), (3, 4), (3, 3))
+    arrivals((0, 5), (3, 0), (3, 1), (0, 6))
     for r in every:
         passed(r, 0)
         m = tiles(src_of(r), 0, 0, mid, low)
         if r == 0:
-            arrivals((3, 5), (1, 6), (2, 6))
+            arrivals((0, 7), (1, 4), (2, 4), (1, 5), (2, 5))
         m = tiles(src_of(r), 0, mid, vl, m)
         if r == 0:
-            arrivals((3, 6))
+            arrivals((3, 6), (1, 6), (2, 6), (3, 7))
         finish(src_of(r), 0, m)
-    arrivals((3, 7), (1, 7), (2, 7))
-    for r in every:
-        project(src_of(r), 0)
     with jax.named_scope("ohsum"):
         onehot_sum()
+    arrivals((3, 4), (3, 5), (1, 7), (2, 7))
+    share_out(x, 1)
+    share_out(x, 0)
+    for r in every:
+        share_out(src_of(r), 0)
     for r in every:
         passed(r, 1)
         finish(src_of(r), 1, tiles(src_of(r), 1, 0, vl, low))
+        share_out(src_of(r), 1)
     for r in every:
+        project(src_of(r), 0)
         project(src_of(r), 1)
 
     local = [pltpu.make_async_copy(sv.at[me], rv.at[me], loc_sem.at[0]),

time: 52.8 us -> 50 us (0.947)
  Pallas kernels: 51.3 us -> 48.4 us
    pallas_call x1, Pallas kernels: 51.3 us -> 48.4 us  [on_device(): pl.pallas_call(functools.partial(kernel, nv, nf), out_shape=jax.ShapeDtyp...]
where the time goes in v2:
time: 50 us; the launch traced here: 49.8 us
  Pallas kernels  48.4 us (97%)
  local copies, waits for them, and re-layouts  1.38 us (3%)
    pallas_call x1, Pallas kernels, on_device(): pl.pallas_call(functools.partial(kernel, nv, nf), out_shape=jax.ShapeDtyp...  48.4 us
    unnamed x1, local copies, waits for them, and re-layouts  1.38 us

profile of v2, /device:TPU:0, one launch (start us, length us, event | category | flops | bytes accessed | tf_op | source)
XLA Modules:
  0.0 49.8 jit_solution(2417581293153871024)
XLA Ops:
  0.0 48.4 %shard_map.73 = f32[16,512]{1,0:T(8,128)} custom-call(bf16[256,4096]{1,0:T(8,128)(2,1)} %hid_in.1, bf16[1024,4096]{1,0:T(8,128)(2,1)} %head_in.1, bf16[1024,128]{1,0:T(8,128)(2,1)} %oproj_in.1, bf16[4096,128]{1,0:T(8,128)(2,1)} %iproj_in.1, s32[8,1,128]{2,1,0:T(1,128)} %bitcast.4, s32[8,1,128]{2,1,0:T(1,128)} %bitcast.5, bf16[2048,4096]{1,0:T(8,128)(2,1)} %gs_in.1), custom_call_target="tpu_custom_call" | custom-call | tf_op jit(solution)/shard_map/pallas_call | solution.py:441
  48.4 1.4 %copy.9 = f32[512,16]{0,1:T(8,128)} copy(f32[512,16]{0,1:T(8,128)} %bitcast.3) | data formatting | bytes 65536

commit v3 on v2

--- a/solution.py
+++ b/solution.py
@@ -291,25 +291,25 @@
     arrivals((3, 3), (1, 2), (2, 2))
     with jax.named_scope("over"):
         onehot_over()
-    arrivals((0, 4), (1, 3), (2, 3))
-    project(x, 1)
-    arrivals((0, 5), (3, 0), (3, 1), (0, 6))
+    arrivals((0, 4), (1, 3), (2, 3), (0, 5), (3, 0), (3, 1), (0, 6), (1, 4), (2, 4))
     for r in every:
         passed(r, 0)
         m = tiles(src_of(r), 0, 0, mid, low)
         if r == 0:
-            arrivals((0, 7), (1, 4), (2, 4), (1, 5), (2, 5))
+            arrivals((0, 7))
         m = tiles(src_of(r), 0, mid, vl, m)
         if r == 0:
-            arrivals((3, 6), (1, 6), (2, 6), (3, 7))
+            arrivals((1, 5), (2, 5))
         finish(src_of(r), 0, m)
     with jax.named_scope("ohsum"):
         onehot_sum()
-    arrivals((3, 4), (3, 5), (1, 7), (2, 7))
-    share_out(x, 1)
+    arrivals((3, 6), (1, 6), (2, 6))
+    project(x, 1)
+    arrivals((3, 7), (3, 4), (3, 5), (1, 7), (2, 7))
     share_out(x, 0)
     for r in every:
         share_out(src_of(r), 0)
+    share_out(x, 1)
     for r in every:
         passed(r, 1)
         finish(src_of(r), 1, tiles(src_of(r), 1, 0, vl, low))

time: 50 us -> 49.8 us (level)
  no operation moved by 1% of the time
where the time goes in v3:
time: 49.8 us; the launch traced here: 49.6 us
  Pallas kernels  48.2 us (97%)
  local copies, waits for them, and re-layouts  1.38 us (3%)
    pallas_call x1, Pallas kernels, on_device(): pl.pallas_call(functools.partial(kernel, nv, nf), out_shape=jax.ShapeDtyp...  48.2 us
    unnamed x1, local copies, waits for them, and re-layouts  1.38 us

profile of v3, /device:TPU:0, one launch (start us, length us, event | category | flops | bytes accessed | tf_op | source)
XLA Modules:
  0.0 49.6 jit_solution(15030751606875528671)
XLA Ops:
  0.0 48.2 %shard_map.73 = f32[16,512]{1,0:T(8,128)} custom-call(bf16[256,4096]{1,0:T(8,128)(2,1)} %hid_in.1, bf16[1024,4096]{1,0:T(8,128)(2,1)} %head_in.1, bf16[1024,128]{1,0:T(8,128)(2,1)} %oproj_in.1, bf16[4096,128]{1,0:T(8,128)(2,1)} %iproj_in.1, s32[8,1,128]{2,1,0:T(1,128)} %bitcast.4, s32[8,1,128]{2,1,0:T(1,128)} %bitcast.5, bf16[2048,4096]{1,0:T(8,128)(2,1)} %gs_in.1), custom_call_target="tpu_custom_call" | custom-call | tf_op jit(solution)/shard_map/pallas_call | solution.py:441
  48.2 1.4 %copy.9 = f32[512,16]{0,1:T(8,128)} copy(f32[512,16]{0,1:T(8,128)} %bitcast.3) | data formatting | bytes 65536
